TPU v7x, 128 devices: a whole 4x4x4 slice. The times are simulated.
128 devices in a mesh: irrep: 8 (over z, x_lo), row: 16 (over y, x_hi, core).
Axes of the slice: x: 4 (x_hi: 2, x_lo: 2; x = x_hi * 2 + x_lo), y: 4, z: 4, core: 2. Of those that a mesh axis runs over, the one named last changes fastest.
Arguments:
- densities: float32 [8, 4096, 512], P('irrep', 'row'), may hold values from -6 to 6
- reduced_kernel: float32 [8, 24576, 4096], P('irrep', 'row'), may hold values from -0.09375 to 0.09375
Outputs:
- potentials: float32 [8, 24576, 512], P('irrep', 'row')
All inputs are finite; a program needn't handle non-finite values.
Results may differ from a plain program's by a relative error of at most 0.000086.
Values sent between devices are 32-bit elements; how exact they have to be, the bound alone decides.
A program may use at most 128 MiB of HBM per device.

v0:
```python
import math

import jax
import jax.numpy as jnp
from jax import lax
from jax.sharding import PartitionSpec as P


def partner_2(value, axis, stride):
    mask = 2**stride
    pairs = [(source, source ^ mask) for source in range(lax.axis_size(axis))]
    return lax.ppermute(value, axis, pairs)


def passed_along(block, axis, distance):
    devices = range(lax.axis_size(axis))
    route = [((i - distance) % len(devices), i) for i in devices]
    return lax.ppermute(block, axis, route)


def body(densities, reduced_kernel):
    octants = lax.axis_size("irrep")
    norm_scale = 1.0 / math.sqrt(octants)
    kernel_tile = reduced_kernel[0]
    src_rows = densities.shape[1]
    holding = densities[0]
    octant_index = lax.axis_index("irrep")
    for level in range(octants.bit_length() - 1):
        partner = partner_2(holding, "irrep", level)
        upper_half = octant_index >> level & 1
        holding = jnp.where(upper_half == 1, partner - holding, holding + partner)
    folded = holding * norm_scale

    def product(source_block, start):
        columns = lax.dynamic_slice_in_dim(kernel_tile, start, source_block.shape[0], 1)
        return jnp.dot(
            columns,
            source_block,
            precision=lax.Precision.HIGHEST,
            preferred_element_type=jnp.float32,
        )

    row_index = lax.axis_index("row")
    row_count = lax.axis_size("row")
    first_sum = product(folded, row_index * src_rows)

    def turn(turn_index, carry):
        summed, source_block = carry
        source_block = passed_along(source_block, "row", 1)
        owner = (row_index - turn_index) % row_count
        return (summed + product(source_block, owner * src_rows), source_block)

    summed, last_block = lax.fori_loop(1, row_count, turn, (first_sum, folded))
    return summed[None]


def solution(mesh):
    placed = (P("irrep", "row", None), P("irrep", "row", None))
    return jax.shard_map(
        body, mesh=mesh, in_specs=placed, out_specs=P("irrep", "row", None), check_vma=False
    )
```

profile of v0, /device:TPU:0, one launch (start us, length us, event | category | flops | bytes accessed | tf_op | source)
XLA Modules:
  0.0 337.4 jit_solution(13967788986259217751)
XLA Ops:
  1.6 12.1 %collective-permute-done.1 = f32[256,512]{1,0:T(8,128)S(1)} collective-permute-done((f32[256,512]{1,0:T(8,128)}, f32[256,512]{1,0:T(8,128)S(1)}, u32[]{:S(2)}, u32[]{:S(2)}) %collective-permute-start.1) | collective-permute-done | bytes 524320 | tf_op jit(solution)/shard_map/ppermute | solution.py:12
  14.9 2.2 collective-permute-start.2
  17.1 11.1 %collective-permute-done.2 = f32[256,512]{1,0:T(8,128)S(1)} collective-permute-done((f32[256,512]{1,0:T(8,128)S(1)}, f32[256,512]{1,0:T(8,128)S(1)}, u32[]{:S(2)}, u32[]{:S(2)}) %collective-permute-start.2) | collective-permute-done | bytes 524320 | tf_op jit(solution)/shard_map/ppermute | solution.py:12
  28.3 3.8 %collective-permute-start.3 = (f32[256,512]{1,0:T(8,128)S(1)}, f32[256,512]{1,0:T(8,128)S(1)}, u32[]{:S(2)}, u32[]{:S(2)}) collective-permute-start(f32[256,512]{1,0:T(8,128)S(1)} %add_select_fusion), channel_id=1, source_target_pairs={{0,64},{16,80},{32,96},{48,112},{64,0},{80,16},{96,32},{112,48},{1... | collective-permute-start | bytes 1572872 | tf_op jit(solution)/shard_map/ppermute | solution.py:12
  32.1 10.7 %collective-permute-done.3 = f32[256,512]{1,0:T(8,128)S(1)} collective-permute-done((f32[256,512]{1,0:T(8,128)S(1)}, f32[256,512]{1,0:T(8,128)S(1)}, u32[]{:S(2)}, u32[]{:S(2)}) %collective-permute-start.3) | collective-permute-done | bytes 524320 | tf_op jit(solution)/shard_map/ppermute | solution.py:12
  42.9 4.3 %fusion.2 = f32[1536,512]{1,0:T(8,128)S(1)} fusion(f32[256,512]{1,0:T(8,128)S(1)} %select_multiply_fusion, f32[1,1536,4096]{2,1,0:T(8,128)} %param.5, s32[]{:T(128)S(6)} %select_n.53), kind=kOutput, calls=%fused_computation.3 | convolution fusion | flops 2415919104 | bytes 5242884 | tf_op jit(solution)/shard_map/dot_general | solution.py:36
  47.1 288.5 %while.17 = (s32[]{:T(128)}, f32[1536,512]{1,0:T(8,128)S(1)}, f32[256,512]{1,0:T(8,128)}, s32[]{:T(128)}, f32[1536,4096]{1,0:T(8,128)}, /*index=5*/s32[]{:T(128)...) while((s32[]{:T(128)}, f32[1536,512]{1,0:T(8,128)S(1)}, f32[256,512]{1,0:T(8,128)}, ...), condition=%wide.region_1.2_spmd, body=%wide.region_0.1_spmd.sunk | while | flops 2416705536 | bytes 11534656 | solution.py:53
  47.3 12.5 %collective-permute-done = f32[256,512]{1,0:T(8,128)} collective-permute-done((f32[256,512]{1,0:T(8,128)}, f32[256,512]{1,0:T(8,128)}, u32[]{:S(2)}, u32[]{:S(2)}) %collective-permute-start) | collective-permute-done | bytes 524320 | tf_op jit(solution)/shard_map/while/body/eval_jaxpr/ppermute | solution.py:18
  59.7 1.9 copy.11
  61.6 4.7 %convolution_add_fusion.2 = f32[1536,512]{1,0:T(8,128)S(1)} fusion(f32[1536,512]{1,0:T(8,128)S(1)} %get-tuple-element.192, f32[256,512]{1,0:T(8,128)} %collective-permute-done, f32[1536,4096]{1,0:T(8,128)} %get-tuple-element.206, s32[]{:T(128)S(6)} %select_n.69), kind=kOutput, calls=%fused_computation.clone.1 | convolution fusion | flops 2416705536 | bytes 8388612 | tf_op jit(solution)/shard_map/while/body/eval_jaxpr/dot_general | solution.py:36
  66.5 12.5 %collective-permute-done = f32[256,512]{1,0:T(8,128)} collective-permute-done((f32[256,512]{1,0:T(8,128)}, f32[256,512]{1,0:T(8,128)}, u32[]{:S(2)}, u32[]{:S(2)}) %collective-permute-start) | collective-permute-done | bytes 524320 | tf_op jit(solution)/shard_map/while/body/eval_jaxpr/ppermute | solution.py:18
  79.0 1.9 copy.11
  80.9 4.7 %convolution_add_fusion.2 = f32[1536,512]{1,0:T(8,128)S(1)} fusion(f32[1536,512]{1,0:T(8,128)S(1)} %get-tuple-element.192, f32[256,512]{1,0:T(8,128)} %collective-permute-done, f32[1536,4096]{1,0:T(8,128)} %get-tuple-element.206, s32[]{:T(128)S(6)} %select_n.69), kind=kOutput, calls=%fused_computation.clone.1 | convolution fusion | flops 2416705536 | bytes 8388612 | tf_op jit(solution)/shard_map/while/body/eval_jaxpr/dot_general | solution.py:36
  85.7 12.5 %collective-permute-done = f32[256,512]{1,0:T(8,128)} collective-permute-done((f32[256,512]{1,0:T(8,128)}, f32[256,512]{1,0:T(8,128)}, u32[]{:S(2)}, u32[]{:S(2)}) %collective-permute-start) | collective-permute-done | bytes 524320 | tf_op jit(solution)/shard_map/while/body/eval_jaxpr/ppermute | solution.py:18
  98.2 1.9 copy.11
  100.1 4.7 %convolution_add_fusion.2 = f32[1536,512]{1,0:T(8,128)S(1)} fusion(f32[1536,512]{1,0:T(8,128)S(1)} %get-tuple-element.192, f32[256,512]{1,0:T(8,128)} %collective-permute-done, f32[1536,4096]{1,0:T(8,128)} %get-tuple-element.206, s32[]{:T(128)S(6)} %select_n.69), kind=kOutput, calls=%fused_computation.clone.1 | convolution fusion | flops 2416705536 | bytes 8388612 | tf_op jit(solution)/shard_map/while/body/eval_jaxpr/dot_general | solution.py:36
  105.0 12.5 %collective-permute-done = f32[256,512]{1,0:T(8,128)} collective-permute-done((f32[256,512]{1,0:T(8,128)}, f32[256,512]{1,0:T(8,128)}, u32[]{:S(2)}, u32[]{:S(2)}) %collective-permute-start) | collective-permute-done | bytes 524320 | tf_op jit(solution)/shard_map/while/body/eval_jaxpr/ppermute | solution.py:18
  117.5 1.9 copy.11
  119.3 4.7 %convolution_add_fusion.2 = f32[1536,512]{1,0:T(8,128)S(1)} fusion(f32[1536,512]{1,0:T(8,128)S(1)} %get-tuple-element.192, f32[256,512]{1,0:T(8,128)} %collective-permute-done, f32[1536,4096]{1,0:T(8,128)} %get-tuple-element.206, s32[]{:T(128)S(6)} %select_n.69), kind=kOutput, calls=%fused_computation.clone.1 | convolution fusion | flops 2416705536 | bytes 8388612 | tf_op jit(solution)/shard_map/while/body/eval_jaxpr/dot_general | solution.py:36
  124.2 12.5 %collective-permute-done = f32[256,512]{1,0:T(8,128)} collective-permute-done((f32[256,512]{1,0:T(8,128)}, f32[256,512]{1,0:T(8,128)}, u32[]{:S(2)}, u32[]{:S(2)}) %collective-permute-start) | collective-permute-done | bytes 524320 | tf_op jit(solution)/shard_map/while/body/eval_jaxpr/ppermute | solution.py:18
  136.7 1.9 copy.11
  138.6 4.7 %convolution_add_fusion.2 = f32[1536,512]{1,0:T(8,128)S(1)} fusion(f32[1536,512]{1,0:T(8,128)S(1)} %get-tuple-element.192, f32[256,512]{1,0:T(8,128)} %collective-permute-done, f32[1536,4096]{1,0:T(8,128)} %get-tuple-element.206, s32[]{:T(128)S(6)} %select_n.69), kind=kOutput, calls=%fused_computation.clone.1 | convolution fusion | flops 2416705536 | bytes 8388612 | tf_op jit(solution)/shard_map/while/body/eval_jaxpr/dot_general | solution.py:36
  143.4 12.5 %collective-permute-done = f32[256,512]{1,0:T(8,128)} collective-permute-done((f32[256,512]{1,0:T(8,128)}, f32[256,512]{1,0:T(8,128)}, u32[]{:S(2)}, u32[]{:S(2)}) %collective-permute-start) | collective-permute-done | bytes 524320 | tf_op jit(solution)/shard_map/while/body/eval_jaxpr/ppermute | solution.py:18
  157.8 4.7 %convolution_add_fusion.2 = f32[1536,512]{1,0:T(8,128)S(1)} fusion(f32[1536,512]{1,0:T(8,128)S(1)} %get-tuple-element.192, f32[256,512]{1,0:T(8,128)} %collective-permute-done, f32[1536,4096]{1,0:T(8,128)} %get-tuple-element.206, s32[]{:T(128)S(6)} %select_n.69), kind=kOutput, calls=%fused_computation.clone.1 | convolution fusion | flops 2416705536 | bytes 8388612 | tf_op jit(solution)/shard_map/while/body/eval_jaxpr/dot_general | solution.py:36
  162.7 12.5 %collective-permute-done = f32[256,512]{1,0:T(8,128)} collective-permute-done((f32[256,512]{1,0:T(8,128)}, f32[256,512]{1,0:T(8,128)}, u32[]{:S(2)}, u32[]{:S(2)}) %collective-permute-start) | collective-permute-done | bytes 524320 | tf_op jit(solution)/shard_map/while/body/eval_jaxpr/ppermute | solution.py:18
  175.2 1.9 copy.11
  177.0 4.7 %convolution_add_fusion.2 = f32[1536,512]{1,0:T(8,128)S(1)} fusion(f32[1536,512]{1,0:T(8,128)S(1)} %get-tuple-element.192, f32[256,512]{1,0:T(8,128)} %collective-permute-done, f32[1536,4096]{1,0:T(8,128)} %get-tuple-element.206, s32[]{:T(128)S(6)} %select_n.69), kind=kOutput, calls=%fused_computation.clone.1 | convolution fusion | flops 2416705536 | bytes 8388612 | tf_op jit(solution)/shard_map/while/body/eval_jaxpr/dot_general | solution.py:36
  181.9 12.5 %collective-permute-done = f32[256,512]{1,0:T(8,128)} collective-permute-done((f32[256,512]{1,0:T(8,128)}, f32[256,512]{1,0:T(8,128)}, u32[]{:S(2)}, u32[]{:S(2)}) %collective-permute-start) | collective-permute-done | bytes 524320 | tf_op jit(solution)/shard_map/while/body/eval_jaxpr/ppermute | solution.py:18
  194.4 1.9 copy.11
  196.3 4.7 %convolution_add_fusion.2 = f32[1536,512]{1,0:T(8,128)S(1)} fusion(f32[1536,512]{1,0:T(8,128)S(1)} %get-tuple-element.192, f32[256,512]{1,0:T(8,128)} %collective-permute-done, f32[1536,4096]{1,0:T(8,128)} %get-tuple-element.206, s32[]{:T(128)S(6)} %select_n.69), kind=kOutput, calls=%fused_computation.clone.1 | convolution fusion | flops 2416705536 | bytes 8388612 | tf_op jit(solution)/shard_map/while/body/eval_jaxpr/dot_general | solution.py:36
  201.1 12.5 %collective-permute-done = f32[256,512]{1,0:T(8,128)} collective-permute-done((f32[256,512]{1,0:T(8,128)}, f32[256,512]{1,0:T(8,128)}, u32[]{:S(2)}, u32[]{:S(2)}) %collective-permute-start) | collective-permute-done | bytes 524320 | tf_op jit(solution)/shard_map/while/body/eval_jaxpr/ppermute | solution.py:18
  213.6 1.9 copy.11
  215.5 4.7 %convolution_add_fusion.2 = f32[1536,512]{1,0:T(8,128)S(1)} fusion(f32[1536,512]{1,0:T(8,128)S(1)} %get-tuple-element.192, f32[256,512]{1,0:T(8,128)} %collective-permute-done, f32[1536,4096]{1,0:T(8,128)} %get-tuple-element.206, s32[]{:T(128)S(6)} %select_n.69), kind=kOutput, calls=%fused_computation.clone.1 | convolution fusion | flops 2416705536 | bytes 8388612 | tf_op jit(solution)/shard_map/while/body/eval_jaxpr/dot_general | solution.py:36
  220.4 12.5 %collective-permute-done = f32[256,512]{1,0:T(8,128)} collective-permute-done((f32[256,512]{1,0:T(8,128)}, f32[256,512]{1,0:T(8,128)}, u32[]{:S(2)}, u32[]{:S(2)}) %collective-permute-start) | collective-permute-done | bytes 524320 | tf_op jit(solution)/shard_map/while/body/eval_jaxpr/ppermute | solution.py:18
  232.9 1.9 copy.11
  234.7 4.7 %convolution_add_fusion.2 = f32[1536,512]{1,0:T(8,128)S(1)} fusion(f32[1536,512]{1,0:T(8,128)S(1)} %get-tuple-element.192, f32[256,512]{1,0:T(8,128)} %collective-permute-done, f32[1536,4096]{1,0:T(8,128)} %get-tuple-element.206, s32[]{:T(128)S(6)} %select_n.69), kind=kOutput, calls=%fused_computation.clone.1 | convolution fusion | flops 2416705536 | bytes 8388612 | tf_op jit(solution)/shard_map/while/body/eval_jaxpr/dot_general | solution.py:36
  239.6 12.5 %collective-permute-done = f32[256,512]{1,0:T(8,128)} collective-permute-done((f32[256,512]{1,0:T(8,128)}, f32[256,512]{1,0:T(8,128)}, u32[]{:S(2)}, u32[]{:S(2)}) %collective-permute-start) | collective-permute-done | bytes 524320 | tf_op jit(solution)/shard_map/while/body/eval_jaxpr/ppermute | solution.py:18
  254.0 4.7 %convolution_add_fusion.2 = f32[1536,512]{1,0:T(8,128)S(1)} fusion(f32[1536,512]{1,0:T(8,128)S(1)} %get-tuple-element.192, f32[256,512]{1,0:T(8,128)} %collective-permute-done, f32[1536,4096]{1,0:T(8,128)} %get-tuple-element.206, s32[]{:T(128)S(6)} %select_n.69), kind=kOutput, calls=%fused_computation.clone.1 | convolution fusion | flops 2416705536 | bytes 8388612 | tf_op jit(solution)/shard_map/while/body/eval_jaxpr/dot_general | solution.py:36
  258.8 12.5 %collective-permute-done = f32[256,512]{1,0:T(8,128)} collective-permute-done((f32[256,512]{1,0:T(8,128)}, f32[256,512]{1,0:T(8,128)}, u32[]{:S(2)}, u32[]{:S(2)}) %collective-permute-start) | collective-permute-done | bytes 524320 | tf_op jit(solution)/shard_map/while/body/eval_jaxpr/ppermute | solution.py:18
  271.3 1.9 copy.11
  273.2 4.7 %convolution_add_fusion.2 = f32[1536,512]{1,0:T(8,128)S(1)} fusion(f32[1536,512]{1,0:T(8,128)S(1)} %get-tuple-element.192, f32[256,512]{1,0:T(8,128)} %collective-permute-done, f32[1536,4096]{1,0:T(8,128)} %get-tuple-element.206, s32[]{:T(128)S(6)} %select_n.69), kind=kOutput, calls=%fused_computation.clone.1 | convolution fusion | flops 2416705536 | bytes 8388612 | tf_op jit(solution)/shard_map/while/body/eval_jaxpr/dot_general | solution.py:36
  278.1 12.5 %collective-permute-done = f32[256,512]{1,0:T(8,128)} collective-permute-done((f32[256,512]{1,0:T(8,128)}, f32[256,512]{1,0:T(8,128)}, u32[]{:S(2)}, u32[]{:S(2)}) %collective-permute-start) | collective-permute-done | bytes 524320 | tf_op jit(solution)/shard_map/while/body/eval_jaxpr/ppermute | solution.py:18
  290.6 1.9 copy.11
  292.4 4.7 %convolution_add_fusion.2 = f32[1536,512]{1,0:T(8,128)S(1)} fusion(f32[1536,512]{1,0:T(8,128)S(1)} %get-tuple-element.192, f32[256,512]{1,0:T(8,128)} %collective-permute-done, f32[1536,4096]{1,0:T(8,128)} %get-tuple-element.206, s32[]{:T(128)S(6)} %select_n.69), kind=kOutput, calls=%fused_computation.clone.1 | convolution fusion | flops 2416705536 | bytes 8388612 | tf_op jit(solution)/shard_map/while/body/eval_jaxpr/dot_general | solution.py:36
  297.3 12.5 %collective-permute-done = f32[256,512]{1,0:T(8,128)} collective-permute-done((f32[256,512]{1,0:T(8,128)}, f32[256,512]{1,0:T(8,128)}, u32[]{:S(2)}, u32[]{:S(2)}) %collective-permute-start) | collective-permute-done | bytes 524320 | tf_op jit(solution)/shard_map/while/body/eval_jaxpr/ppermute | solution.py:18
  311.7 4.7 %convolution_add_fusion.2 = f32[1536,512]{1,0:T(8,128)S(1)} fusion(f32[1536,512]{1,0:T(8,128)S(1)} %get-tuple-element.192, f32[256,512]{1,0:T(8,128)} %collective-permute-done, f32[1536,4096]{1,0:T(8,128)} %get-tuple-element.206, s32[]{:T(128)S(6)} %select_n.69), kind=kOutput, calls=%fused_computation.clone.1 | convolution fusion | flops 2416705536 | bytes 8388612 | tf_op jit(solution)/shard_map/while/body/eval_jaxpr/dot_general | solution.py:36
  316.6 12.5 %collective-permute-done = f32[256,512]{1,0:T(8,128)} collective-permute-done((f32[256,512]{1,0:T(8,128)}, f32[256,512]{1,0:T(8,128)}, u32[]{:S(2)}, u32[]{:S(2)}) %collective-permute-start) | collective-permute-done | bytes 524320 | tf_op jit(solution)/shard_map/while/body/eval_jaxpr/ppermute | solution.py:18
  330.9 4.7 %convolution_add_fusion.2 = f32[1536,512]{1,0:T(8,128)S(1)} fusion(f32[1536,512]{1,0:T(8,128)S(1)} %get-tuple-element.192, f32[256,512]{1,0:T(8,128)} %collective-permute-done, f32[1536,4096]{1,0:T(8,128)} %get-tuple-element.206, s32[]{:T(128)S(6)} %select_n.69), kind=kOutput, calls=%fused_computation.clone.1 | convolution fusion | flops 2416705536 | bytes 8388612 | tf_op jit(solution)/shard_map/while/body/eval_jaxpr/dot_general | solution.py:36
  (27 shorter events, 13.2 us)
Async XLA Ops:
  0.0 13.7 %collective-permute-start.1 = (f32[256,512]{1,0:T(8,128)}, f32[256,512]{1,0:T(8,128)S(1)}, u32[]{:S(2)}, u32[]{:S(2)}) collective-permute-start(f32[256,512]{1,0:T(8,128)} %bitcast.12), channel_id=1, source_target_pairs={{0,16},{16,0},{32,48},{48,32},{64,80},{80,64},{96,112},{112,96},{1... | collective-permute-start | bytes 1572872 | tf_op jit(solution)/shard_map/ppermute | solution.py:12
  14.9 13.3 %collective-permute-start.2 = (f32[256,512]{1,0:T(8,128)S(1)}, f32[256,512]{1,0:T(8,128)S(1)}, u32[]{:S(2)}, u32[]{:S(2)}) collective-permute-start(f32[256,512]{1,0:T(8,128)S(1)} %add_select_fusion.1), channel_id=1, source_target_pairs={{0,32},{16,48},{32,0},{48,16},{64,96},{80,112},{96,64},{112,80},{1... | collective-permute-start | bytes 1572872 | tf_op jit(solution)/shard_map/ppermute | solution.py:12
  28.3 14.4 %collective-permute-start.3 = (f32[256,512]{1,0:T(8,128)S(1)}, f32[256,512]{1,0:T(8,128)S(1)}, u32[]{:S(2)}, u32[]{:S(2)}) collective-permute-start(f32[256,512]{1,0:T(8,128)S(1)} %add_select_fusion), channel_id=1, source_target_pairs={{0,64},{16,80},{32,96},{48,112},{64,0},{80,16},{96,32},{112,48},{1... | collective-permute-start | bytes 1572872 | tf_op jit(solution)/shard_map/ppermute | solution.py:12
  42.8 4.3 %copy-start.1 = (f32[256,512]{1,0:T(8,128)}, f32[256,512]{1,0:T(8,128)S(1)}, u32[]{:S(2)}) copy-start(f32[256,512]{1,0:T(8,128)S(1)} %select_multiply_fusion) | copy-start | bytes 1572868
  47.1 12.6 %collective-permute-start = (f32[256,512]{1,0:T(8,128)}, f32[256,512]{1,0:T(8,128)}, u32[]{:S(2)}, u32[]{:S(2)}) collective-permute-start(f32[256,512]{1,0:T(8,128)} %get-tuple-element.193), channel_id=1, source_target_pairs={{15,0},{0,1},{1,2},{2,3},{3,4},{4,5},{5,6},{6,7},{7,8},{8,9},{9,10... | collective-permute-start | bytes 1572872 | tf_op jit(solution)/shard_map/while/body/eval_jaxpr/ppermute | solution.py:18
  66.4 12.6 %collective-permute-start = (f32[256,512]{1,0:T(8,128)}, f32[256,512]{1,0:T(8,128)}, u32[]{:S(2)}, u32[]{:S(2)}) collective-permute-start(f32[256,512]{1,0:T(8,128)} %get-tuple-element.193), channel_id=1, source_target_pairs={{15,0},{0,1},{1,2},{2,3},{3,4},{4,5},{5,6},{6,7},{7,8},{8,9},{9,10... | collective-permute-start | bytes 1572872 | tf_op jit(solution)/shard_map/while/body/eval_jaxpr/ppermute | solution.py:18
  85.6 12.6 %collective-permute-start = (f32[256,512]{1,0:T(8,128)}, f32[256,512]{1,0:T(8,128)}, u32[]{:S(2)}, u32[]{:S(2)}) collective-permute-start(f32[256,512]{1,0:T(8,128)} %get-tuple-element.193), channel_id=1, source_target_pairs={{15,0},{0,1},{1,2},{2,3},{3,4},{4,5},{5,6},{6,7},{7,8},{8,9},{9,10... | collective-permute-start | bytes 1572872 | tf_op jit(solution)/shard_map/while/body/eval_jaxpr/ppermute | solution.py:18
  104.8 12.6 %collective-permute-start = (f32[256,512]{1,0:T(8,128)}, f32[256,512]{1,0:T(8,128)}, u32[]{:S(2)}, u32[]{:S(2)}) collective-permute-start(f32[256,512]{1,0:T(8,128)} %get-tuple-element.193), channel_id=1, source_target_pairs={{15,0},{0,1},{1,2},{2,3},{3,4},{4,5},{5,6},{6,7},{7,8},{8,9},{9,10... | collective-permute-start | bytes 1572872 | tf_op jit(solution)/shard_map/while/body/eval_jaxpr/ppermute | solution.py:18
  124.1 12.6 %collective-permute-start = (f32[256,512]{1,0:T(8,128)}, f32[256,512]{1,0:T(8,128)}, u32[]{:S(2)}, u32[]{:S(2)}) collective-permute-start(f32[256,512]{1,0:T(8,128)} %get-tuple-element.193), channel_id=1, source_target_pairs={{15,0},{0,1},{1,2},{2,3},{3,4},{4,5},{5,6},{6,7},{7,8},{8,9},{9,10... | collective-permute-start | bytes 1572872 | tf_op jit(solution)/shard_map/while/body/eval_jaxpr/ppermute | solution.py:18
  143.3 12.6 %collective-permute-start = (f32[256,512]{1,0:T(8,128)}, f32[256,512]{1,0:T(8,128)}, u32[]{:S(2)}, u32[]{:S(2)}) collective-permute-start(f32[256,512]{1,0:T(8,128)} %get-tuple-element.193), channel_id=1, source_target_pairs={{15,0},{0,1},{1,2},{2,3},{3,4},{4,5},{5,6},{6,7},{7,8},{8,9},{9,10... | collective-permute-start | bytes 1572872 | tf_op jit(solution)/shard_map/while/body/eval_jaxpr/ppermute | solution.py:18
  162.6 12.6 %collective-permute-start = (f32[256,512]{1,0:T(8,128)}, f32[256,512]{1,0:T(8,128)}, u32[]{:S(2)}, u32[]{:S(2)}) collective-permute-start(f32[256,512]{1,0:T(8,128)} %get-tuple-element.193), channel_id=1, source_target_pairs={{15,0},{0,1},{1,2},{2,3},{3,4},{4,5},{5,6},{6,7},{7,8},{8,9},{9,10... | collective-permute-start | bytes 1572872 | tf_op jit(solution)/shard_map/while/body/eval_jaxpr/ppermute | solution.py:18
  181.8 12.6 %collective-permute-start = (f32[256,512]{1,0:T(8,128)}, f32[256,512]{1,0:T(8,128)}, u32[]{:S(2)}, u32[]{:S(2)}) collective-permute-start(f32[256,512]{1,0:T(8,128)} %get-tuple-element.193), channel_id=1, source_target_pairs={{15,0},{0,1},{1,2},{2,3},{3,4},{4,5},{5,6},{6,7},{7,8},{8,9},{9,10... | collective-permute-start | bytes 1572872 | tf_op jit(solution)/shard_map/while/body/eval_jaxpr/ppermute | solution.py:18
  201.0 12.6 %collective-permute-start = (f32[256,512]{1,0:T(8,128)}, f32[256,512]{1,0:T(8,128)}, u32[]{:S(2)}, u32[]{:S(2)}) collective-permute-start(f32[256,512]{1,0:T(8,128)} %get-tuple-element.193), channel_id=1, source_target_pairs={{15,0},{0,1},{1,2},{2,3},{3,4},{4,5},{5,6},{6,7},{7,8},{8,9},{9,10... | collective-permute-start | bytes 1572872 | tf_op jit(solution)/shard_map/while/body/eval_jaxpr/ppermute | solution.py:18
  220.3 12.6 %collective-permute-start = (f32[256,512]{1,0:T(8,128)}, f32[256,512]{1,0:T(8,128)}, u32[]{:S(2)}, u32[]{:S(2)}) collective-permute-start(f32[256,512]{1,0:T(8,128)} %get-tuple-element.193), channel_id=1, source_target_pairs={{15,0},{0,1},{1,2},{2,3},{3,4},{4,5},{5,6},{6,7},{7,8},{8,9},{9,10... | collective-permute-start | bytes 1572872 | tf_op jit(solution)/shard_map/while/body/eval_jaxpr/ppermute | solution.py:18
  239.5 12.6 %collective-permute-start = (f32[256,512]{1,0:T(8,128)}, f32[256,512]{1,0:T(8,128)}, u32[]{:S(2)}, u32[]{:S(2)}) collective-permute-start(f32[256,512]{1,0:T(8,128)} %get-tuple-element.193), channel_id=1, source_target_pairs={{15,0},{0,1},{1,2},{2,3},{3,4},{4,5},{5,6},{6,7},{7,8},{8,9},{9,10... | collective-permute-start | bytes 1572872 | tf_op jit(solution)/shard_map/while/body/eval_jaxpr/ppermute | solution.py:18
  258.7 12.6 %collective-permute-start = (f32[256,512]{1,0:T(8,128)}, f32[256,512]{1,0:T(8,128)}, u32[]{:S(2)}, u32[]{:S(2)}) collective-permute-start(f32[256,512]{1,0:T(8,128)} %get-tuple-element.193), channel_id=1, source_target_pairs={{15,0},{0,1},{1,2},{2,3},{3,4},{4,5},{5,6},{6,7},{7,8},{8,9},{9,10... | collective-permute-start | bytes 1572872 | tf_op jit(solution)/shard_map/while/body/eval_jaxpr/ppermute | solution.py:18
  278.0 12.6 %collective-permute-start = (f32[256,512]{1,0:T(8,128)}, f32[256,512]{1,0:T(8,128)}, u32[]{:S(2)}, u32[]{:S(2)}) collective-permute-start(f32[256,512]{1,0:T(8,128)} %get-tuple-element.193), channel_id=1, source_target_pairs={{15,0},{0,1},{1,2},{2,3},{3,4},{4,5},{5,6},{6,7},{7,8},{8,9},{9,10... | collective-permute-start | bytes 1572872 | tf_op jit(solution)/shard_map/while/body/eval_jaxpr/ppermute | solution.py:18
  297.2 12.6 %collective-permute-start = (f32[256,512]{1,0:T(8,128)}, f32[256,512]{1,0:T(8,128)}, u32[]{:S(2)}, u32[]{:S(2)}) collective-permute-start(f32[256,512]{1,0:T(8,128)} %get-tuple-element.193), channel_id=1, source_target_pairs={{15,0},{0,1},{1,2},{2,3},{3,4},{4,5},{5,6},{6,7},{7,8},{8,9},{9,10... | collective-permute-start | bytes 1572872 | tf_op jit(solution)/shard_map/while/body/eval_jaxpr/ppermute | solution.py:18
  316.4 12.6 %collective-permute-start = (f32[256,512]{1,0:T(8,128)}, f32[256,512]{1,0:T(8,128)}, u32[]{:S(2)}, u32[]{:S(2)}) collective-permute-start(f32[256,512]{1,0:T(8,128)} %get-tuple-element.193), channel_id=1, source_target_pairs={{15,0},{0,1},{1,2},{2,3},{3,4},{4,5},{5,6},{6,7},{7,8},{8,9},{9,10... | collective-permute-start | bytes 1572872 | tf_op jit(solution)/shard_map/while/body/eval_jaxpr/ppermute | solution.py:18
  335.7 1.7 copy-start
where the time goes:
time: 339 us; the launch traced here: 337 us
  waiting for transfers between devices  221 us (65%)
  matrix products  75.4 us (22%)
  local copies, waits for them, and re-layouts  29.7 us (9%)
  starting transfers between devices  8.78 us (3%)
    ppermute x15, waiting for transfers between devices, passed_along(): return lax.ppermute(block, axis, route)  187 us
    dot_general x16, matrix products, product(): jnp.dot(columns, source_block, precision=lax.Precision.HIGHEST, preferred...  75.4 us
    ppermute x3, waiting for transfers between devices, partner_2(): return lax.ppermute(value, axis, pairs)  33.8 us
    while x15, local copies, waits for them, and re-layouts  28 us
    ppermute x3, starting transfers between devices, partner_2(): return lax.ppermute(value, axis, pairs)  7.63 us
  transfers between devices with their start and end apart: 18, of which 18 were waited for; matrix products, arithmetic and copies ran while one was open for 0% of the time, Pallas kernels for 0%

commit v1 on v0

v1 whole, which is shorter than its diff:
```python
import math

import jax
import jax.numpy as jnp
from jax import lax
from jax.experimental import pallas as pl
from jax.experimental.pallas import tpu as pltpu
from jax.sharding import PartitionSpec as P

F32, BF16 = jnp.float32, jnp.bfloat16
MESH = pl.DeviceIdType.MESH
HALF = 256

SLOTS = ("00", "30", "10", "01", "20", "31", "11", "21")
SLOT = {name: i for i, name in enumerate(SLOTS)}

UNIT_ROWS = (64, 64, 64, 64)
PIECE = 128
FIRST_PRODUCT = 10.0
SPLIT_PRODUCT = True


def units_of(rows):
    units = []
    for q in range(2):
        start = 0
        for count in rows:
            units.append((q, start, count))
            start += count
    return units


def plan(units, piece, first_product, split):
    link_rate, core_rate = 94e3, 440e3
    hop, two_hops, on_chip = 1.6, 2.4, 0.9
    steps, copies = {}, {}

    def cover(q, start, count):
        return [u for u, (uq, a, n) in enumerate(units) if uq == q and a < start + count and start < a + n]

    pieces = [(q, start) for q in range(2) for start in range(0, HALF, piece)]
    for u, (q, start, count) in enumerate(units):
        for flow in ("L1", "L2", "L3", "yp", "ym", "x2"):
            link = {"L1": "xi", "L2": "zA", "L3": "zB"}.get(flow, flow)
            copies[(flow, u)] = (link, count * HALF * 4)
        steps[("A1", u)] = (0, [("L1", u)], [], 0.1, [("L2", u)])
        steps[("A2", u)] = (0, [("L2", u)], [("A1", u)], 0.1, [("L3", u)])
        steps[("A3", u)] = (0, [("L3", u)], [("A2", u)], 0.1, [("x2", u), ("yp", u), ("ym", u)])
    for q, start in pieces:
        parts = cover(q, start, piece)
        size = piece * HALF * 4
        source = ("ym", "yp")[q]
        copies[("F", q, start)] = (source, size)
        steps[("FW", q, start)] = (1, [(source, u) for u in parts], [], 0.05, [("F", q, start)])
        copies[("CP", q, start)] = ("yp", size)
        copies[("CM", q, start)] = ("ym", size)
        steps[("XC", q, start)] = (
            2,
            [("x2", u) for u in parts],
            [("FW", *p) for p in pieces],
            0.05,
            [("CP", q, start), ("CM", q, start)],
        )
        copies[("X2", q, start)] = ("x2", size)
        steps[("XX", q, start)] = (1, [("F", q, start)], [], 0.05, [("X2", q, start)])
    for q in range(2):
        whole = cover(q, 0, HALF)
        half = [(q, start) for start in range(0, HALF, piece)]
        arrivals = {
            "00": [],
            "30": [("yp", u) for u in whole],
            "10": [("ym", u) for u in whole],
            "01": [("x2", u) for u in whole],
            "20": [("F", *p) for p in half],
            "31": [("CP", *p) for p in half],
            "11": [("CM", *p) for p in half],
            "21": [("X2", *p) for p in half],
        }
        for slot, needed in arrivals.items():
            before = [("A3", u) for u in whole] if slot == "00" else []
            share = ("S", slot, q)
            copies[share] = ("core", HALF * HALF * 4)
            steps[("SH", slot, q)] = (3, needed, before, 0.05, [share])
            if split:
                steps[("G0", slot, q)] = (5, needed, before, 0.7, [])
                steps[("G1", slot, q)] = (5, [share], [("SH", slot, q)], 0.7, [])
            else:
                steps[("G", slot, q)] = (5, [share], [("SH", slot, q)], 1.31, [])

    free, arrival, done, order = {}, {}, {}, []

    def issue(copy, now):
        flow, size = copies[copy]
        link = "xi" if flow == "x2" else flow
        wire = size / core_rate if flow == "core" else 2 * size / link_rate
        latency = {"core": on_chip, "x2": two_hops}.get(flow, hop)
        free[link] = max(now, free.get(link, 0.0)) + wire
        arrival[copy] = free[link] + latency

    now = 1.0
    for u in range(len(units)):
        issue(("L1", u), now)
    while len(order) < len(steps):
        best = None
        for name, (rank, needed, before, length, sends) in steps.items():
            if name in done or any(b not in done for b in before) or any(n not in arrival for n in needed):
                continue
            ready = max([arrival[n] for n in needed] + [done[b] for b in before] + [0.0])
            if rank == 5:
                ready = max(ready, first_product)
            key = (max(ready, now), rank if ready <= now else 9, ready)
            if best is None or key < best[0]:
                best = (key, name, ready)
        name = best[1]
        now = max(now, best[2]) + steps[name][3]
        done[name] = now
        order.append(name)
        for copy in steps[name][4]:
            issue(copy, now)
    return order, steps, list(copies)


UNITS = units_of(UNIT_ROWS)
ORDER, STEPS, COPIES = plan(UNITS, PIECE, FIRST_PRODUCT, SPLIT_PRODUCT)
COPY_AT = {name: i for i, name in enumerate(COPIES)}


def split_bf16(x):
    high = x.astype(BF16)
    return high, (x - high.astype(F32)).astype(BF16)


def kernel(d_ref, k_ref, o_ref, own, got1, fold1, got2, keep2, give2, got3, gathered, tiles, total, send_sem, recv_sem, own_sem, tile_sem, out_sem):
    c, r = lax.axis_index("irrep"), lax.axis_index("row")
    x_lo, z0, z1 = c % 2, c // 2 % 2, c // 4
    core, x_hi, y = r % 2, r // 2 % 2, r // 4
    to = {
        "xi": (c + 1 - 2 * x_lo, r),
        "zA": (c + 2 - 4 * z0, r),
        "zB": (c + 2 - 4 * z0 + 4 - 8 * z1, r),
        "yp": (c, (r + 4) % 16),
        "ym": (c, (r + 12) % 16),
        "x2": (c, r + 2 - 4 * x_hi),
        "core": (c, r + 1 - 2 * core),
    }
    sign_x = (1 - 2 * x_lo).astype(F32)
    sign_z0 = (1 - 2 * z0).astype(F32)
    sign_z1 = (1 - 2 * z1).astype(F32)
    scale = 1.0 / math.sqrt(8)

    own_copy = pltpu.make_async_copy(d_ref.at[0], own, own_sem)
    own_copy.start()
    barrier = pltpu.get_barrier_semaphore()
    for target in to.values():
        pl.semaphore_signal(barrier, 1, device_id=target, device_id_type=MESH)
    pl.semaphore_wait(barrier, len(to))

    def part(u):
        q, start, count = UNITS[u]
        return pl.ds(start, count), pl.ds(q * HALF, HALF)

    def block(slot, q, start, count, side=0):
        return gathered.at[SLOT[slot], side, pl.ds(start, count), pl.ds(q * HALF, HALF)]

    def describe(name):
        flow = name[0]
        if flow in ("L1", "L2", "L3", "yp", "ym", "x2"):
            u = name[1]
            rows, cols = part(u)
            q, start, count = UNITS[u]
        if flow == "L1":
            source, target, link = d_ref.at[0, rows, cols], got1.at[rows, cols], "xi"
        elif flow == "L2":
            source, target, link = fold1.at[rows, cols], got2.at[rows, cols], "zA"
        elif flow == "L3":
            source, target, link = give2.at[rows, cols], got3.at[rows, cols], "zB"
        elif flow in ("yp", "ym", "x2"):
            slot = {"yp": "30", "ym": "10", "x2": "01"}[flow]
            source, target, link = block("00", q, start, count), block(slot, q, start, count), flow
        elif flow == "S":
            source, target, link = block(name[1], name[2], 0, HALF), block(name[1], name[2], 0, HALF, 1), "core"
        else:
            _, q, start = name
            origin, slot, link = {
                "F": (("10", "30")[q], "20", ("ym", "yp")[q]),
                "CP": ("01", "31", "yp"),
                "CM": ("01", "11", "ym"),
                "X2": ("20", "21", "x2"),
            }[flow]
            source, target = block(origin, q, start, PIECE), block(slot, q, start, PIECE)
        i = COPY_AT[name]
        return pltpu.make_async_remote_copy(
            src_ref=source,
            dst_ref=target,
            send_sem=send_sem.at[i],
            recv_sem=recv_sem.at[i],
            device_id=to[link],
            device_id_type=MESH,
        )

    arrived = set()

    def wait_for(names):
        for name in names:
            if name not in arrived:
                arrived.add(name)
                describe(name).wait_recv()

    for u in range(len(UNITS)):
        describe(("L1", u)).start()
    tile_copies = []
    for i, slot in enumerate(SLOTS):
        block_at = ((y + int(slot[0])) % 4 * 2 + (x_hi + int(slot[1])) % 2) * 2
        for side in range(2):
            owner = block_at + (core + side) % 2
            copy = pltpu.make_async_copy(
                k_ref.at[0, :, pl.ds(pl.multiple_of(owner * HALF, HALF), HALF)],
                tiles.at[2 * i + side],
                tile_sem.at[2 * i + side],
            )
            copy.start()
            tile_copies.append(copy)
    own_copy.wait()

    tiles_in, started = set(), set()

    def product(slot, q, sides):
        left, right = [], []
        for side in sides:
            i = 2 * SLOT[slot] + side
            if i not in tiles_in:
                tiles_in.add(i)
                tile_copies[i].wait()
            high, low = split_bf16(tiles[i])
            b_high, b_low = split_bf16(gathered[SLOT[slot], side, :, q * HALF : (q + 1) * HALF])
            left += [high, low, high]
            right += [b_high, b_high, b_low]
        term = jnp.dot(jnp.concatenate(left, 1), jnp.concatenate(right, 0), preferred_element_type=F32)
        cols = pl.ds(q * HALF, HALF)
        if q in started:
            total[:, cols] += term
        else:
            started.add(q)
            total[:, cols] = term

    left_over = {q: sum(1 for s in STEPS if s[0][0] == "G" and s[2] == q) for q in range(2)}
    out_copies = []
    for name in ORDER:
        kind = name[0]
        _, needed, _, _, sends = STEPS[name]
        wait_for(needed)
        if kind in ("A1", "A2", "A3"):
            rows, cols = part(name[1])
            if kind == "A1":
                fold1[rows, cols] = got1[rows, cols] + sign_x * own[rows, cols]
            elif kind == "A2":
                mine, other = fold1[rows, cols], got2[rows, cols]
                give2[rows, cols] = mine - sign_z0 * other
                keep2[rows, cols] = other + sign_z0 * mine
            else:
                value = (got3[rows, cols] + sign_z1 * keep2[rows, cols]) * scale
                gathered[SLOT["00"], 0, rows, cols] = value
        for copy in sends:
            describe(copy).start()
        if kind[0] == "G":
            slot, q = name[1:]
            product(slot, q, {"G0": (0,), "G1": (1,), "G": (0, 1)}[kind])
            left_over[q] -= 1
            if left_over[q] == 0:
                cols = pl.ds(q * HALF, HALF)
                copy = pltpu.make_async_copy(total.at[:, cols], o_ref.at[0, :, cols], out_sem.at[q])
                copy.start()
                out_copies.append(copy)
    wait_for(COPIES)
    for name in COPIES:
        describe(name).wait_send()
    for copy in out_copies:
        copy.wait()


def body(densities, reduced_kernel):
    rows = reduced_kernel.shape[1]
    stage = pltpu.VMEM((HALF, 2 * HALF), F32)
    return pl.pallas_call(
        kernel,
        out_shape=jax.ShapeDtypeStruct((1, rows, 2 * HALF), F32),
        in_specs=[pl.BlockSpec(memory_space=pl.ANY)] * 2,
        out_specs=pl.BlockSpec(memory_space=pl.ANY),
        scratch_shapes=[stage] * 7
        + [
            pltpu.VMEM((8, 2, HALF, 2 * HALF), F32),
            pltpu.VMEM((16, rows, HALF), F32),
            pltpu.VMEM((rows, 2 * HALF), F32),
            pltpu.SemaphoreType.DMA((len(COPIES),)),
            pltpu.SemaphoreType.DMA((len(COPIES),)),
            pltpu.SemaphoreType.DMA,
            pltpu.SemaphoreType.DMA((16,)),
            pltpu.SemaphoreType.DMA((2,)),
        ],
        compiler_params=pltpu.CompilerParams(
            collective_id=0, has_side_effects=True, vmem_limit_bytes=63 * 2**20
        ),
        name="fold_gather_product",
    )(densities, reduced_kernel)


def solution(mesh):
    placed = (P("irrep", "row", None), P("irrep", "row", None))
    return jax.shard_map(
        body, mesh=mesh, in_specs=placed, out_specs=P("irrep", "row", None), check_vma=False
    )
```

time: 339 us -> 73.8 us (0.22)
  waiting for transfers between devices: 221 us -> 0 us
  matrix products: 75.4 us -> 0 us
  Pallas kernels: 0 us -> 68.7 us
  local copies, waits for them, and re-layouts: 29.7 us -> 3.86 us
  starting transfers between devices: 8.78 us -> 0 us
    ppermute x18 -> x0, waiting for transfers between devices: 221 us -> none  [the longest x15 187 us: passed_along(): return lax.ppermute(block, axis, route)]
    dot_general x16 -> x0, matrix products: 75.4 us -> none  [product(): jnp.dot(columns, source_block, precision=lax.Precision.HIGHEST, preferred...]
    pallas_call x0 -> x1, Pallas kernels: none -> 68.7 us  [body(): pl.pallas_call(kernel, out_shape=jax.ShapeDtypeStruct((1, rows, 2 * HALF)...]
    while x15 -> x0, local copies, waits for them, and re-layouts: 28 us -> none
    ppermute x18 -> x0, starting transfers between devices: 8.78 us -> none  [the longest x3 7.63 us: partner_2(): return lax.ppermute(value, axis, pairs)]
  transfers between devices with their start and end apart: 18 -> 0, of which waited for: 18 -> 0; matrix products, arithmetic and copies ran while one was open for 0% -> 0% of each run, Pallas kernels for 0% -> 0%
where the time goes in v1:
time: 73.8 us; the launch traced here: 72.6 us
  Pallas kernels  68.7 us (93%)
  local copies, waits for them, and re-layouts  3.86 us (5%)
    pallas_call x1, Pallas kernels, body(): pl.pallas_call(kernel, out_shape=jax.ShapeDtypeStruct((1, rows, 2 * HALF)...  68.7 us
    unnamed x1, local copies, waits for them, and re-layouts  3.86 us

profile of v1, /device:TPU:0, one launch (start us, length us, event | category | flops | bytes accessed | tf_op | source)
XLA Modules:
  0.0 72.6 jit_solution(8781917819683859821)
XLA Ops:
  0.0 68.7 %fold_gather_product.1 = f32[1,1536,512]{2,1,0:T(8,128)} custom-call(f32[1,256,512]{2,1,0:T(8,128)} %d_ref.1, f32[1,1536,4096]{2,1,0:T(8,128)} %k_ref.1), custom_call_target="tpu_custom_call" | custom-call | tf_op jit(solution)/shard_map/fold_gather_product/pallas_call | solution.py:284
  68.7 3.9 %copy.4 = f32[1,1536,512]{2,1,0:T(8,128)} copy(f32[1,1536,512]{2,1,0:T(8,128)} %fold_gather_product.1) | data formatting | bytes 6291456

commit v2 on v1

v2 whole, which is shorter than its diff:
```python
import math

import jax
import jax.numpy as jnp
from jax import lax
from jax.experimental import pallas as pl
from jax.experimental.pallas import tpu as pltpu
from jax.sharding import PartitionSpec as P

F32, BF16 = jnp.float32, jnp.bfloat16
MESH = pl.DeviceIdType.MESH
HALF = 256

SLOTS = ("00", "30", "10", "01", "20", "31", "11", "21")
SLOT = {name: i for i, name in enumerate(SLOTS)}

UNIT_ROWS = ((32,) * 8, (64,) * 4)

RANK = {"A1": 1.3, "A2": 1.6, "A3": -1.8, "FY": 0.2, "FC": 2.5, "XC": 1.1, "SH": 3.9, "G": 6}
FIRST_PRODUCT, FIRST_CROSSED = 0.0, 33.0


def units_of(rows):
    units = []
    for q in range(2):
        start = 0
        for count in rows[q]:
            units.append((q, start, count))
            start += count
    return units


def graph(units):
    steps, copies, landing = {}, {}, {}
    for u, (q, start, count) in enumerate(units):
        along, against = (("YP", "YM"), ("YM", "YP"))[u % 2]
        links = {
            "L1": "xi",
            "L2": "zA",
            "L3": "zB",
            "X": "x2",
            "YP": "yp",
            "YM": "ym",
            "CP": "yp",
            "CM": "ym",
            "FY": along.lower(),
            "FC": "x2",
        }
        for flow, link in links.items():
            copies[(flow, u)] = (link, count * HALF * 4)
        steps[("A1", u)] = ("A1", [("L1", u)], [], 0.15, [("L2", u)])
        steps[("A2", u)] = ("A2", [("L2", u)], [("A1", u)], 0.15, [("L3", u)])
        steps[("A3", u)] = ("A3", [("L3", u)], [("A2", u)], 0.15, [("X", u), ("YP", u), ("YM", u)])
        steps[("FY", u)] = ("FY", [(along, u)], [], 0.05, [("FY", u)])
        steps[("XC", u)] = ("XC", [("X", u)], [], 0.05, [("CP", u), ("CM", u)])
        steps[("FC", u)] = ("FC", [("FY", u)], [], 0.05, [("FC", u)])
        flows = {"00": None, "30": "YP", "10": "YM", "01": "X", "20": "FY", "31": "CP", "11": "CM", "21": "FC"}
        for slot, flow in flows.items():
            arrivals, before = landing.setdefault((slot, q), ([], []))
            if flow is None:
                before.append(("A3", u))
            else:
                arrivals.append((flow, u))
    for (slot, q), (arrivals, before) in landing.items():
        copies[("S", slot, q)] = ("core", HALF * HALF * 4)
        steps[("SH", slot, q)] = ("SH", arrivals, before, 0.05, [("S", slot, q)])
        steps[("G0", slot, q)] = ("G", arrivals, before, 0.85, [])
        steps[("G1", slot, q)] = ("G", [("S", slot, q)], [("SH", slot, q)], 0.85, [])
    return steps, copies


def plan(units, steps, copies):
    latency = {"xi": 1.97, "zA": 1.95, "zB": 3.4, "yp": 3.1, "ym": 3.1, "x2": 4.7, "core": 2.0}
    free, arrival, done, order = {}, {}, {}, []

    def issue(copy, now):
        flow, size = copies[copy]
        link = "xi" if flow == "x2" else flow
        wire = size / 440e3 if flow == "core" else 2 * size / 90.6e3
        free[link] = max(now, free.get(link, 0.0)) + wire
        arrival[copy] = free[link] + latency[flow]

    now = 5.3
    for u in range(len(units)):
        issue(("L1", u), now)
    while len(order) < len(steps):
        best = None
        for name, (kind, needed, before, length, sends) in steps.items():
            if name in done or any(b not in done for b in before) or any(n not in arrival for n in needed):
                continue
            ready = max([arrival[n] for n in needed] + [done[b] for b in before] + [0.0])
            ready = max(ready, {"G": FIRST_PRODUCT, "XC": FIRST_CROSSED}.get(kind, 0.0))
            key = (max(ready, now), RANK[kind] if ready <= now else 9, ready)
            if best is None or key < best[0]:
                best = (key, name, ready)
        name = best[1]
        now = max(now, best[2]) + steps[name][3]
        done[name] = now
        order.append(name)
        for copy in steps[name][4]:
            now += 0.03
            issue(copy, now)
    return order


UNITS = units_of(UNIT_ROWS)
STEPS, COPIES = graph(UNITS)
ORDER = plan(UNITS, STEPS, COPIES)
COPY_AT = {name: i for i, name in enumerate(COPIES)}


def split_bf16(x):
    high = x.astype(BF16)
    return high, (x - high.astype(F32)).astype(BF16)


def kernel(d_ref, k_ref, o_ref, got1, fold1, got2, keep2, give2, got3, gathered, tiles, send_sem, recv_sem, tile_sem):
    c, r = lax.axis_index("irrep"), lax.axis_index("row")
    x_lo, z0, z1 = c % 2, c // 2 % 2, c // 4
    core, x_hi, y = r % 2, r // 2 % 2, r // 4
    to = {
        "xi": (c + 1 - 2 * x_lo, r),
        "zA": (c + 2 - 4 * z0, r),
        "zB": (c + 2 - 4 * z0 + 4 - 8 * z1, r),
        "yp": (c, (r + 4) % 16),
        "ym": (c, (r + 12) % 16),
        "x2": (c, r + 2 - 4 * x_hi),
        "core": (c, r + 1 - 2 * core),
    }
    sign_x = (1 - 2 * x_lo).astype(F32)
    sign_z0 = (1 - 2 * z0).astype(F32)
    sign_z1 = (1 - 2 * z1).astype(F32)
    scale = 1.0 / math.sqrt(8)

    barrier = pltpu.get_barrier_semaphore()
    for target in to.values():
        pl.semaphore_signal(barrier, 1, device_id=target, device_id_type=MESH)
    pl.semaphore_wait(barrier, len(to))

    def part(u):
        q, start, count = UNITS[u]
        return pl.ds(start, count), pl.ds(q * HALF, HALF)

    def block(slot, q, start, count, side=0):
        return gathered.at[SLOT[slot], side, pl.ds(start, count), pl.ds(q * HALF, HALF)]

    def describe(name):
        flow = name[0]
        link = COPIES[name][0]
        if flow == "S":
            source, target = block(name[1], name[2], 0, HALF), block(name[1], name[2], 0, HALF, 1)
        else:
            u = name[1]
            rows, cols = part(u)
            source, target = {
                "L1": lambda: (d_ref.at[0, rows, cols], got1.at[rows, cols]),
                "L2": lambda: (fold1.at[rows, cols], got2.at[rows, cols]),
                "L3": lambda: (give2.at[rows, cols], got3.at[rows, cols]),
                "X": lambda: (block("00", *UNITS[u]), block("01", *UNITS[u])),
                "YP": lambda: (block("00", *UNITS[u]), block("30", *UNITS[u])),
                "YM": lambda: (block("00", *UNITS[u]), block("10", *UNITS[u])),
                "FY": lambda: (block(("30", "10")[u % 2], *UNITS[u]), block("20", *UNITS[u])),
                "CP": lambda: (block("01", *UNITS[u]), block("31", *UNITS[u])),
                "CM": lambda: (block("01", *UNITS[u]), block("11", *UNITS[u])),
                "FC": lambda: (block("20", *UNITS[u]), block("21", *UNITS[u])),
            }[flow]()
        i = COPY_AT[name]
        return pltpu.make_async_remote_copy(
            src_ref=source,
            dst_ref=target,
            send_sem=send_sem.at[i],
            recv_sem=recv_sem.at[i],
            device_id=to[link],
            device_id_type=MESH,
        )

    arrived = set()

    def wait_for(names):
        for name in names:
            if name not in arrived:
                arrived.add(name)
                describe(name).wait_recv()

    for u in range(len(UNITS)):
        describe(("L1", u)).start()
    tile_copies = []
    for i, slot in enumerate(SLOTS):
        block_at = ((y + int(slot[0])) % 4 * 2 + (x_hi + int(slot[1])) % 2) * 2
        for side in range(2):
            owner = block_at + (core + side) % 2
            copy = pltpu.make_async_copy(
                k_ref.at[0, :, pl.ds(pl.multiple_of(owner * HALF, HALF), HALF)],
                tiles.at[2 * i + side],
                tile_sem.at[2 * i + side],
            )
            copy.start()
            tile_copies.append(copy)

    tiles_in = set()

    def run(name):
        kind, needed, _, _, sends = STEPS[name]
        wait_for(needed)
        if kind in ("A1", "A2", "A3"):
            rows, cols = part(name[1])
            if kind == "A1":
                fold1[rows, cols] = got1[rows, cols] + sign_x * d_ref[0, rows, cols]
            elif kind == "A2":
                mine, other = fold1[rows, cols], got2[rows, cols]
                give2[rows, cols] = mine - sign_z0 * other
                keep2[rows, cols] = other + sign_z0 * mine
            else:
                value = (got3[rows, cols] + sign_z1 * keep2[rows, cols]) * scale
                gathered[SLOT["00"], 0, rows, cols] = value
        for copy in sends:
            describe(copy).start()
        if kind == "G":
            i = tile_of(name)
            if i not in tiles_in:
                tiles_in.add(i)
                tile_copies[i].wait()

    def tile_of(name):
        return 2 * SLOT[name[1]] + int(name[0][1])

    products = [name for name in ORDER if name[0][0] == "G"]
    blocks, block_steps = [], []
    for name in ORDER:
        block_steps.append(name)
        if name[0][0] == "G":
            blocks.append(block_steps)
            block_steps = []
    assert not block_steps

    for name in blocks[0]:
        run(name)
    o_ref[...] = jnp.zeros_like(o_ref)

    @pl.loop(0, len(products))
    def _(g):
        def pick(low, high):
            if high - low == 1:
                if low:
                    for name in blocks[low]:
                        run(name)
                name = products[low]
                return jnp.int32(tile_of(name)), jnp.int32(name[2])
            middle = (low + high) // 2
            return lax.cond(g < middle, lambda: pick(low, middle), lambda: pick(middle, high))

        i, q = pick(0, len(products))
        cols = pl.ds(pl.multiple_of(q * HALF, HALF), HALF)
        high, low = split_bf16(tiles[i])
        b_high, b_low = split_bf16(gathered[i // 2, i % 2, :, cols])
        o_ref[0, :, cols] += jnp.dot(
            jnp.concatenate([high, low, high], 1),
            jnp.concatenate([b_high, b_high, b_low], 0),
            preferred_element_type=F32,
        )

    wait_for(COPIES)
    for name in COPIES:
        describe(name).wait_send()


def body(densities, reduced_kernel):
    rows = reduced_kernel.shape[1]
    stage = pltpu.VMEM((HALF, 2 * HALF), F32)
    return pl.pallas_call(
        kernel,
        out_shape=jax.ShapeDtypeStruct((1, rows, 2 * HALF), F32),
        in_specs=[pl.BlockSpec(memory_space=pltpu.VMEM), pl.BlockSpec(memory_space=pl.ANY)],
        out_specs=pl.BlockSpec(memory_space=pltpu.VMEM),
        scratch_shapes=[stage] * 6
        + [
            pltpu.VMEM((8, 2, HALF, 2 * HALF), F32),
            pltpu.VMEM((16, rows, HALF), F32),
            pltpu.SemaphoreType.DMA((len(COPIES),)),
            pltpu.SemaphoreType.DMA((len(COPIES),)),
            pltpu.SemaphoreType.DMA((16,)),
        ],
        compiler_params=pltpu.CompilerParams(
            collective_id=0, has_side_effects=True, vmem_limit_bytes=50 * 2**20
        ),
        name="fold_gather_product",
    )(densities, reduced_kernel)


def solution(mesh):
    placed = (P("irrep", "row", None), P("irrep", "row", None))
    return jax.shard_map(
        body, mesh=mesh, in_specs=placed, out_specs=P("irrep", "row", None), check_vma=False
    )
```

time: 73.8 us -> 59.9 us (0.81); the launches traced: 72.6 us -> 59.8 us
  Pallas kernels: 68.7 us -> 57.1 us
  local copies, waits for them, and re-layouts: 3.86 us -> 2.71 us
    pallas_call x1, Pallas kernels: 68.7 us -> 57.1 us  [body(): pl.pallas_call(kernel, out_shape=jax.ShapeDtypeStruct((1, rows, 2 * HALF)...]
    unnamed x1 -> x3, local copies, waits for them, and re-layouts: 3.86 us -> 2.71 us
where the time goes in v2:
time: 59.9 us; the launch traced here: 59.8 us
  Pallas kernels  57.1 us (95%)
  local copies, waits for them, and re-layouts  2.71 us (5%)
    pallas_call x1, Pallas kernels, body(): pl.pallas_call(kernel, out_shape=jax.ShapeDtypeStruct((1, rows, 2 * HALF)...  57.1 us
    unnamed x3, local copies, waits for them, and re-layouts  2.71 us

profile of v2, /device:TPU:0, one launch (start us, length us, event | category | flops | bytes accessed | tf_op | source)
XLA Modules:
  0.0 59.8 jit_solution(10539021131716041628)
XLA Ops:
  0.0 0.0 copy-start
  0.0 1.0 %copy-done = f32[1,256,512]{2,1,0:T(8,128)S(1)} copy-done((f32[1,256,512]{2,1,0:T(8,128)S(1)}, f32[1,256,512]{2,1,0:T(8,128)}, u32[]{:S(2)}) %copy-start) | copy-done | bytes 524312
  1.0 57.1 %fold_gather_product.1 = f32[1,1536,512]{2,1,0:T(8,128)S(1)} custom-call(f32[1,256,512]{2,1,0:T(8,128)S(1)} %copy-done, f32[1,1536,4096]{2,1,0:T(8,128)} %k_ref.1), custom_call_target="tpu_custom_call" | custom-call | tf_op jit(solution)/shard_map/fold_gather_product/pallas_call | solution.py:270
  58.1 1.7 %copy.4 = f32[1,1536,512]{2,1,0:T(8,128)} copy(f32[1,1536,512]{2,1,0:T(8,128)S(1)} %fold_gather_product.1) | data formatting | bytes 6291456
Async XLA Ops:
  0.0 1.0 %copy-start = (f32[1,256,512]{2,1,0:T(8,128)S(1)}, f32[1,256,512]{2,1,0:T(8,128)}, u32[]{:S(2)}) copy-start(f32[1,256,512]{2,1,0:T(8,128)} %d_ref.1) | copy-start | bytes 1572868

commit v3 on v2

--- a/solution.py
+++ b/solution.py
@@ -16,8 +16,10 @@
 
 UNIT_ROWS = ((32,) * 8, (64,) * 4)
 
-RANK = {"A1": 1.3, "A2": 1.6, "A3": -1.8, "FY": 0.2, "FC": 2.5, "XC": 1.1, "SH": 3.9, "G": 6}
-FIRST_PRODUCT, FIRST_CROSSED = 0.0, 33.0
+RANK = {"A1": 0.88, "A2": 2.27, "A3": 0.54, "FY": 0.3, "FC": 0.5, "XC": 1.75, "XP": 3.92, "XM": 3.92, "SH": 5.32, "G": 6}
+FIRST_PRODUCT, FIRST_CROSSED = 0.0, 30.0
+
+OVER_X = (2, 3)
 
 
 def units_of(rows):
@@ -41,8 +43,8 @@
             "X": "x2",
             "YP": "yp",
             "YM": "ym",
-            "CP": "yp",
-            "CM": "ym",
+            "CP": "x2" if u in OVER_X else "yp",
+            "CM": "x2" if u in OVER_X else "ym",
             "FY": along.lower(),
             "FC": "x2",
         }
@@ -52,7 +54,11 @@
         steps[("A2", u)] = ("A2", [("L2", u)], [("A1", u)], 0.15, [("L3", u)])
         steps[("A3", u)] = ("A3", [("L3", u)], [("A2", u)], 0.15, [("X", u), ("YP", u), ("YM", u)])
         steps[("FY", u)] = ("FY", [(along, u)], [], 0.05, [("FY", u)])
-        steps[("XC", u)] = ("XC", [("X", u)], [], 0.05, [("CP", u), ("CM", u)])
+        if u in OVER_X:
+            steps[("XP", u)] = ("XP", [("YP", u)], [], 0.05, [("CP", u)])
+            steps[("XM", u)] = ("XM", [("YM", u)], [], 0.05, [("CM", u)])
+        else:
+            steps[("XC", u)] = ("XC", [("X", u)], [], 0.05, [("CP", u), ("CM", u)])
         steps[("FC", u)] = ("FC", [("FY", u)], [], 0.05, [("FC", u)])
         flows = {"00": None, "30": "YP", "10": "YM", "01": "X", "20": "FY", "31": "CP", "11": "CM", "21": "FC"}
         for slot, flow in flows.items():
@@ -64,8 +70,7 @@
     for (slot, q), (arrivals, before) in landing.items():
         copies[("S", slot, q)] = ("core", HALF * HALF * 4)
         steps[("SH", slot, q)] = ("SH", arrivals, before, 0.05, [("S", slot, q)])
-        steps[("G0", slot, q)] = ("G", arrivals, before, 0.85, [])
-        steps[("G1", slot, q)] = ("G", [("S", slot, q)], [("SH", slot, q)], 0.85, [])
+        steps[("G", slot, q)] = ("G", [("S", slot, q)], [("SH", slot, q)], 1.4, [])
     return steps, copies
 
 
@@ -160,8 +165,8 @@
                 "YP": lambda: (block("00", *UNITS[u]), block("30", *UNITS[u])),
                 "YM": lambda: (block("00", *UNITS[u]), block("10", *UNITS[u])),
                 "FY": lambda: (block(("30", "10")[u % 2], *UNITS[u]), block("20", *UNITS[u])),
-                "CP": lambda: (block("01", *UNITS[u]), block("31", *UNITS[u])),
-                "CM": lambda: (block("01", *UNITS[u]), block("11", *UNITS[u])),
+                "CP": lambda: (block("30" if u in OVER_X else "01", *UNITS[u]), block("31", *UNITS[u])),
+                "CM": lambda: (block("10" if u in OVER_X else "01", *UNITS[u]), block("11", *UNITS[u])),
                 "FC": lambda: (block("20", *UNITS[u]), block("21", *UNITS[u])),
             }[flow]()
         i = COPY_AT[name]
@@ -174,13 +179,19 @@
             device_id_type=MESH,
         )
 
-    arrived = set()
+    arrived, sent = set(), set()
 
     def wait_for(names):
         for name in names:
             if name not in arrived:
                 arrived.add(name)
                 describe(name).wait_recv()
+
+    def wait_sent(names):
+        for name in names:
+            if name not in sent:
+                sent.add(name)
+                describe(name).wait_send()
 
     for u in range(len(UNITS)):
         describe(("L1", u)).start()
@@ -215,14 +226,14 @@
                 gathered[SLOT["00"], 0, rows, cols] = value
         for copy in sends:
             describe(copy).start()
+        if kind == "A3":
+            wait_sent([("L1", name[1]), ("L2", name[1])])
         if kind == "G":
-            i = tile_of(name)
+            i = SLOT[name[1]]
             if i not in tiles_in:
                 tiles_in.add(i)
-                tile_copies[i].wait()
-
-    def tile_of(name):
-        return 2 * SLOT[name[1]] + int(name[0][1])
+                tile_copies[2 * i].wait()
+                tile_copies[2 * i + 1].wait()
 
     products = [name for name in ORDER if name[0][0] == "G"]
     blocks, block_steps = [], []
@@ -233,9 +244,9 @@
             block_steps = []
     assert not block_steps
 
+    o_ref[...] = jnp.zeros_like(o_ref)
     for name in blocks[0]:
         run(name)
-    o_ref[...] = jnp.zeros_like(o_ref)
 
     @pl.loop(0, len(products))
     def _(g):
@@ -245,23 +256,24 @@
                     for name in blocks[low]:
                         run(name)
                 name = products[low]
-                return jnp.int32(tile_of(name)), jnp.int32(name[2])
+                return jnp.int32(SLOT[name[1]]), jnp.int32(name[2])
             middle = (low + high) // 2
             return lax.cond(g < middle, lambda: pick(low, middle), lambda: pick(middle, high))
 
         i, q = pick(0, len(products))
         cols = pl.ds(pl.multiple_of(q * HALF, HALF), HALF)
-        high, low = split_bf16(tiles[i])
-        b_high, b_low = split_bf16(gathered[i // 2, i % 2, :, cols])
+        left, right = [], []
+        for side in range(2):
+            high, low = split_bf16(tiles[2 * i + side])
+            b_high, b_low = split_bf16(gathered[i, side, :, cols])
+            left += [high, low, high]
+            right += [b_high, b_high, b_low]
         o_ref[0, :, cols] += jnp.dot(
-            jnp.concatenate([high, low, high], 1),
-            jnp.concatenate([b_high, b_high, b_low], 0),
-            preferred_element_type=F32,
+            jnp.concatenate(left, 1), jnp.concatenate(right, 0), preferred_element_type=F32
         )
 
     wait_for(COPIES)
-    for name in COPIES:
-        describe(name).wait_send()
+    wait_sent(COPIES)
 
 
 def body(densities, reduced_kernel):

time: 59.9 us -> 58.9 us (0.983); the launches traced: 59.8 us -> 57.9 us
  Pallas kernels: 57.1 us -> 55.2 us
    pallas_call x1, Pallas kernels: 57.1 us -> 55.2 us  [body(): pl.pallas_call(kernel, out_shape=jax.ShapeDtypeStruct((1, rows, 2 * HALF)...]
where the time goes in v3:
time: 58.9 us; the launch traced here: 57.9 us
  Pallas kernels  55.2 us (94%)
  local copies, waits for them, and re-layouts  2.71 us (5%)
    pallas_call x1, Pallas kernels, body(): pl.pallas_call(kernel, out_shape=jax.ShapeDtypeStruct((1, rows, 2 * HALF)...  55.2 us
    unnamed x3, local copies, waits for them, and re-layouts  2.71 us

profile of v3, /device:TPU:0, one launch (start us, length us, event | category | flops | bytes accessed | tf_op | source)
XLA Modules:
  0.0 57.9 jit_solution(12989339995662671057)
XLA Ops:
  0.0 0.0 copy-start
  0.0 1.0 %copy-done = f32[1,256,512]{2,1,0:T(8,128)S(1)} copy-done((f32[1,256,512]{2,1,0:T(8,128)S(1)}, f32[1,256,512]{2,1,0:T(8,128)}, u32[]{:S(2)}) %copy-start) | copy-done | bytes 524312
  1.0 55.2 %fold_gather_product.1 = f32[1,1536,512]{2,1,0:T(8,128)S(1)} custom-call(f32[1,256,512]{2,1,0:T(8,128)S(1)} %copy-done, f32[1,1536,4096]{2,1,0:T(8,128)} %k_ref.1), custom_call_target="tpu_custom_call" | custom-call | tf_op jit(solution)/shard_map/fold_gather_product/pallas_call | solution.py:282
  56.2 1.7 %copy.4 = f32[1,1536,512]{2,1,0:T(8,128)} copy(f32[1,1536,512]{2,1,0:T(8,128)S(1)} %fold_gather_product.1) | data formatting | bytes 6291456
Async XLA Ops:
  0.0 1.0 %copy-start = (f32[1,256,512]{2,1,0:T(8,128)S(1)}, f32[1,256,512]{2,1,0:T(8,128)}, u32[]{:S(2)}) copy-start(f32[1,256,512]{2,1,0:T(8,128)} %d_ref.1) | copy-start | bytes 1572868

commit v4 on v3

--- a/solution.py
+++ b/solution.py
@@ -16,10 +16,10 @@
 
 UNIT_ROWS = ((32,) * 8, (64,) * 4)
 
-RANK = {"A1": 0.88, "A2": 2.27, "A3": 0.54, "FY": 0.3, "FC": 0.5, "XC": 1.75, "XP": 3.92, "XM": 3.92, "SH": 5.32, "G": 6}
-FIRST_PRODUCT, FIRST_CROSSED = 0.0, 30.0
-
-OVER_X = (2, 3)
+RANK = {"A1": 0.19, "A2": 2.02, "A3": -0.64, "FY": 3.74, "FC": 2.59, "XC": 4.73, "XP": 0.52, "XM": 0.52, "SH": 4.19, "G": 6}
+FIRST_PRODUCT, FIRST_CROSSED = 26.0, 28.0
+
+OVER_X = (2, 3, 6)
 
 
 def units_of(rows):
@@ -70,7 +70,7 @@
     for (slot, q), (arrivals, before) in landing.items():
         copies[("S", slot, q)] = ("core", HALF * HALF * 4)
         steps[("SH", slot, q)] = ("SH", arrivals, before, 0.05, [("S", slot, q)])
-        steps[("G", slot, q)] = ("G", [("S", slot, q)], [("SH", slot, q)], 1.4, [])
+        steps[("G", slot, q)] = ("G", [("S", slot, q)], [("SH", slot, q)], 1.55, [])
     return steps, copies
 
 

time: 58.9 us -> 57.6 us (0.978); the launches traced: 57.9 us -> 57.5 us
  no operation moved by 1% of the time
where the time goes in v4:
time: 57.6 us; the launch traced here: 57.5 us
  Pallas kernels  54.8 us (95%)
  local copies, waits for them, and re-layouts  2.71 us (5%)
    pallas_call x1, Pallas kernels, body(): pl.pallas_call(kernel, out_shape=jax.ShapeDtypeStruct((1, rows, 2 * HALF)...  54.8 us
    unnamed x3, local copies, waits for them, and re-layouts  2.71 us

profile of v4, /device:TPU:0, one launch (start us, length us, event | category | flops | bytes accessed | tf_op | source)
XLA Modules:
  0.0 57.5 jit_solution(14832325389138365154)
XLA Ops:
  0.0 0.0 copy-start
  0.0 1.0 %copy-done = f32[1,256,512]{2,1,0:T(8,128)S(1)} copy-done((f32[1,256,512]{2,1,0:T(8,128)S(1)}, f32[1,256,512]{2,1,0:T(8,128)}, u32[]{:S(2)}) %copy-start) | copy-done | bytes 524312
  1.0 54.8 %fold_gather_product.1 = f32[1,1536,512]{2,1,0:T(8,128)S(1)} custom-call(f32[1,256,512]{2,1,0:T(8,128)S(1)} %copy-done, f32[1,1536,4096]{2,1,0:T(8,128)} %k_ref.1), custom_call_target="tpu_custom_call" | custom-call | tf_op jit(solution)/shard_map/fold_gather_product/pallas_call | solution.py:282
  55.8 1.7 %copy.4 = f32[1,1536,512]{2,1,0:T(8,128)} copy(f32[1,1536,512]{2,1,0:T(8,128)S(1)} %fold_gather_product.1) | data formatting | bytes 6291456
Async XLA Ops:
  0.0 1.0 %copy-start = (f32[1,256,512]{2,1,0:T(8,128)S(1)}, f32[1,256,512]{2,1,0:T(8,128)}, u32[]{:S(2)}) copy-start(f32[1,256,512]{2,1,0:T(8,128)} %d_ref.1) | copy-start | bytes 1572868

commit v5 on v4

--- a/solution.py
+++ b/solution.py
@@ -14,12 +14,12 @@
 SLOTS = ("00", "30", "10", "01", "20", "31", "11", "21")
 SLOT = {name: i for i, name in enumerate(SLOTS)}
 
-UNIT_ROWS = ((32,) * 8, (64,) * 4)
+UNIT_ROWS = ((16, 16, 32, 32, 32, 32, 32, 32, 32), (64,) * 4)
 
 RANK = {"A1": 0.19, "A2": 2.02, "A3": -0.64, "FY": 3.74, "FC": 2.59, "XC": 4.73, "XP": 0.52, "XM": 0.52, "SH": 4.19, "G": 6}
-FIRST_PRODUCT, FIRST_CROSSED = 26.0, 28.0
-
-OVER_X = (2, 3, 6)
+FIRST_PRODUCT, FIRST_CROSSED = 22.0, 28.0
+
+OVER_X = (3, 4, 7)
 
 
 def units_of(rows):

time: 57.6 us -> 58.7 us (1.019)
  no operation moved by 1% of the time
where the time goes in v5:
time: 58.7 us; the launch traced here: 58 us
  Pallas kernels  55.3 us (94%)
  local copies, waits for them, and re-layouts  2.71 us (5%)
    pallas_call x1, Pallas kernels, body(): pl.pallas_call(kernel, out_shape=jax.ShapeDtypeStruct((1, rows, 2 * HALF)...  55.3 us
    unnamed x3, local copies, waits for them, and re-layouts  2.71 us

profile of v5, /device:TPU:0, one launch (start us, length us, event | category | flops | bytes accessed | tf_op | source)
XLA Modules:
  0.0 58.0 jit_solution(11254378867286387191)
XLA Ops:
  0.0 0.0 copy-start
  0.0 1.0 %copy-done = f32[1,256,512]{2,1,0:T(8,128)S(1)} copy-done((f32[1,256,512]{2,1,0:T(8,128)S(1)}, f32[1,256,512]{2,1,0:T(8,128)}, u32[]{:S(2)}) %copy-start) | copy-done | bytes 524312
  1.0 55.3 %fold_gather_product.1 = f32[1,1536,512]{2,1,0:T(8,128)S(1)} custom-call(f32[1,256,512]{2,1,0:T(8,128)S(1)} %copy-done, f32[1,1536,4096]{2,1,0:T(8,128)} %k_ref.1), custom_call_target="tpu_custom_call" | custom-call | tf_op jit(solution)/shard_map/fold_gather_product/pallas_call | solution.py:282
  56.4 1.7 %copy.4 = f32[1,1536,512]{2,1,0:T(8,128)} copy(f32[1,1536,512]{2,1,0:T(8,128)S(1)} %fold_gather_product.1) | data formatting | bytes 6291456
Async XLA Ops:
  0.0 1.0 %copy-start = (f32[1,256,512]{2,1,0:T(8,128)S(1)}, f32[1,256,512]{2,1,0:T(8,128)}, u32[]{:S(2)}) copy-start(f32[1,256,512]{2,1,0:T(8,128)} %d_ref.1) | copy-start | bytes 1572868
